TPU v7x, 32 devices: a whole 2x2x4 slice. The times are simulated.
32 devices in a mesh: ax: 16 (over z, y, x), az: 2 (over core).
Axes of the slice: x: 2, y: 2, z: 4, core: 2. Of those that a mesh axis runs over, the one named last changes fastest.
Arguments:
- source: bfloat16 [2048, 512, 256], P(('ax', 'az')), may hold values from -6 to 6
- forcing: bfloat16 [2048, 512, 256], P(('ax', 'az')), may hold values from -6 to 6
- radial_basis: bfloat16 [128, 256, 256], P('az'), may hold values from -0.375 to 0.375
- eigenvalues: float32 [128, 256], P('az'), may hold values from 0.25 to 16
- radial_weight: float32 [256], replicated, may hold values from 0.5 to 2
Outputs:
- pressure: bfloat16 [2048, 512, 256], P(('ax', 'az'))
- velocity: bfloat16 [2048, 512, 256], P(('ax', 'az'))
All inputs are finite; a program needn't handle non-finite values.
Results may differ from a plain program's by a relative error of at most 0.012.
Values may be sent and summed in bfloat16 or wider, within the bound.
A program may use at most 256 MiB of HBM per device.

v0:
```python
import math

import jax
import jax.numpy as jnp
from jax import lax
from jax.sharding import PartitionSpec as P

NZ = 2048
NTH = 512
KZ = 1024
NC = 256


VISCOUS = 0.5


def fourier_table(coef_count, point_count):
    slot_index = jnp.arange(coef_count, dtype=jnp.int32)
    frequency = jnp.where(slot_index == 1, coef_count // 2, slot_index // 2)
    sine_row = (slot_index % 2 == 1) & (slot_index != 1)
    grid_points = jnp.arange(point_count, dtype=jnp.int32)
    phase_index = frequency[:, None] * grid_points[None, :] % point_count
    angles = phase_index.astype(jnp.float32) * (2.0 * math.pi / point_count)
    table_values = jnp.where(sine_row[:, None], jnp.sin(angles), jnp.cos(angles)) * math.sqrt(
        2.0 / point_count
    )
    return table_values.astype(jnp.bfloat16)


def radial_solve(source_hat, forcing_hat, basis_rows, weighted_rows, eigen_rows):
    kz_count = source_hat.shape[0]
    kz_index = jnp.arange(kz_count, dtype=jnp.int32)
    wavenumber = (kz_index // 2).astype(jnp.float32) * (8.0 / KZ)
    wave_sq = (wavenumber * wavenumber)[:, None, None]
    transformed = jnp.einsum(
        "kcr,crj->kcj", source_hat, weighted_rows, preferred_element_type=jnp.float32
    )
    scaled = (transformed / (eigen_rows[None] + wave_sq)).astype(jnp.bfloat16)
    pressure_full = jnp.einsum(
        "kcj,crj->kcr", scaled, basis_rows, preferred_element_type=jnp.float32
    )
    paired = pressure_full.reshape((kz_count // 2, 2) + pressure_full.shape[1:])
    pair_wave = wavenumber.reshape(kz_count // 2, 2)[:, 0][:, None, None]
    gradient = jnp.stack([pair_wave * paired[:, 1], -pair_wave * paired[:, 0]], axis=1).reshape(
        pressure_full.shape
    )
    helm_rhs = (forcing_hat.astype(jnp.float32) - gradient).astype(jnp.bfloat16)
    transformed_visc = jnp.einsum(
        "kcr,crj->kcj", helm_rhs, weighted_rows, preferred_element_type=jnp.float32
    )
    scaled_visc = (transformed_visc / (1.0 + VISCOUS * (eigen_rows[None] + wave_sq))).astype(
        jnp.bfloat16
    )
    velocity_hat = jnp.einsum(
        "kcj,crj->kcr", scaled_visc, basis_rows, preferred_element_type=jnp.float32
    ).astype(jnp.bfloat16)
    return (pressure_full.astype(jnp.bfloat16), velocity_hat)


def per_device(source, forcing, radial_basis, eigenvalues, radial_weight):
    ax_count = lax.axis_size("ax")
    az_count = lax.axis_size("az")
    az_table = fourier_table(NC, NTH)
    axial_table = fourier_table(KZ, NZ)
    source_coef = jnp.einsum(
        "ct,ztr->zcr", az_table, source, preferred_element_type=jnp.float32
    ).astype(jnp.bfloat16)
    forcing_coef = jnp.einsum(
        "ct,ztr->zcr", az_table, forcing, preferred_element_type=jnp.float32
    ).astype(jnp.bfloat16)
    coef_local = NC // (ax_count * az_count)
    source_cols, forcing_cols = (
        lax.all_to_all(
            lax.all_to_all(source_coef, "az", split_axis=1, concat_axis=0, tiled=True),
            "ax",
            split_axis=1,
            concat_axis=0,
            tiled=True,
        ),
        lax.all_to_all(
            lax.all_to_all(forcing_coef, "az", split_axis=1, concat_axis=0, tiled=True),
            "ax",
            split_axis=1,
            concat_axis=0,
            tiled=True,
        ),
    )
    source_hat = jnp.einsum(
        "kz,zcr->kcr", axial_table, source_cols, preferred_element_type=jnp.float32
    ).astype(jnp.bfloat16)
    forcing_hat = jnp.einsum(
        "kz,zcr->kcr", axial_table, forcing_cols, preferred_element_type=jnp.float32
    ).astype(jnp.bfloat16)
    weighted = (radial_weight[None, :, None] * radial_basis.astype(jnp.float32)).astype(
        jnp.bfloat16
    )
    pair_index = (lax.axis_index("ax") * coef_local + jnp.arange(coef_local, dtype=jnp.int32)) // 2
    pressure_hat, velocity_hat = radial_solve(
        source_hat,
        forcing_hat,
        jnp.take(radial_basis, pair_index, axis=0),
        jnp.take(weighted, pair_index, axis=0),
        jnp.take(eigenvalues, pair_index, axis=0),
    )
    pressure_cols = jnp.einsum(
        "kz,kcr->zcr", axial_table, pressure_hat, preferred_element_type=jnp.float32
    ).astype(jnp.bfloat16)
    velocity_cols = jnp.einsum(
        "kz,kcr->zcr", axial_table, velocity_hat, preferred_element_type=jnp.float32
    ).astype(jnp.bfloat16)
    pressure_coef, velocity_coef = (
        lax.all_to_all(
            lax.all_to_all(pressure_cols, "ax", split_axis=0, concat_axis=1, tiled=True),
            "az",
            split_axis=0,
            concat_axis=1,
            tiled=True,
        ),
        lax.all_to_all(
            lax.all_to_all(velocity_cols, "ax", split_axis=0, concat_axis=1, tiled=True),
            "az",
            split_axis=0,
            concat_axis=1,
            tiled=True,
        ),
    )
    pressure = jnp.einsum(
        "ct,zcr->ztr", az_table, pressure_coef, preferred_element_type=jnp.float32
    ).astype(jnp.bfloat16)
    velocity = jnp.einsum(
        "ct,zcr->ztr", az_table, velocity_coef, preferred_element_type=jnp.float32
    ).astype(jnp.bfloat16)
    return (pressure, velocity)


def solution(mesh):
    placed = (
        P(("ax", "az"), None, None),
        P(("ax", "az"), None, None),
        P("az", None, None),
        P("az", None),
        P(),
    )
    return jax.shard_map(
        per_device,
        mesh=mesh,
        in_specs=placed,
        out_specs=(P(("ax", "az"), None, None), P(("ax", "az"), None, None)),
        check_vma=False,
    )
```

profile of v0, /device:TPU:29, one launch (start us, length us, event | category | flops | bytes accessed | tf_op | source)
XLA Modules:
  0.0 1033.5 jit_solution(1523914847758688512)
XLA Ops:
  0.6 0.0 copy-start
  0.7 0.0 copy-start.5
  0.7 0.0 copy-start.3
  0.7 14.6 %convert_bitcast_fusion.3 = bf16[64,256,256]{2,1,0:T(8,128)(2,1)} fusion(bf16[64,512,256]{2,1,0:T(8,128)(2,1)} %param.7, s32[256]{0:T(256)S(1)} %fusion.93, pred[256]{0:T(512)(128)(4,1)S(1)} %compare_and_fusion.1), kind=kOutput, calls=%fused_computation.27 | convolution fusion | flops 4301389824 | bytes 25167104 | tf_op jit(solution)/shard_map/ct,ztr->zcr/dot_general | solution.py:65
  15.3 11.5 %copy.44 = bf16[64,256,256]{2,0,1:T(8,128)(2,1)} copy(bf16[64,256,256]{2,1,0:T(8,128)(2,1)} %convert_bitcast_fusion.3) | data formatting | bytes 16777216 | tf_op jit(solution)/shard_map/convert_element_type | solution.py:67
  26.9 8.1 all-to-all-start
  35.0 0.0 copy-done.5
  35.0 0.0 copy-done.3
  35.0 14.6 %convert_bitcast_fusion.2 = bf16[64,256,256]{2,1,0:T(8,128)(2,1)} fusion(bf16[64,512,256]{2,1,0:T(8,128)(2,1)} %param.8, s32[256]{0:T(256)S(1)} %fusion.93, pred[256]{0:T(512)(128)(4,1)S(1)} %compare_and_fusion.1), kind=kOutput, calls=%fused_computation.26 | convolution fusion | flops 4301389824 | bytes 25167104 | tf_op jit(solution)/shard_map/ct,ztr->zcr/dot_general | solution.py:68
  49.6 11.4 %copy.58 = bf16[64,256,256]{2,0,1:T(8,128)(2,1)} copy(bf16[64,256,256]{2,1,0:T(8,128)(2,1)} %convert_bitcast_fusion.2) | data formatting | bytes 16777216 | tf_op jit(solution)/shard_map/convert_element_type | solution.py:70
  61.0 0.0 all-to-all-done
  61.0 7.1 all-to-all-start.4
  68.2 11.6 %copy.46 = bf16[2,64,128,256]{3,2,1,0:T(8,128)(2,1)} copy(bf16[2,64,128,256]{3,1,2,0:T(8,128)(2,1)} %bitcast.6) | data formatting | bytes 16777216 | tf_op jit(solution)/shard_map/all_to_all | solution.py:74
  79.8 11.5 %copy.47 = bf16[128,128,256]{2,0,1:T(8,128)(2,1)} copy(bf16[128,128,256]{2,1,0:T(8,128)(2,1)} %bitcast.118) | data formatting | bytes 16777216 | tf_op jit(solution)/shard_map/all_to_all | solution.py:74
  91.3 0.0 all-to-all-done.4
  91.3 6.7 all-to-all-start.1
  98.1 11.6 %copy.60 = bf16[2,64,128,256]{3,2,1,0:T(8,128)(2,1)} copy(bf16[2,64,128,256]{3,1,2,0:T(8,128)(2,1)} %bitcast.25) | data formatting | bytes 16777216 | tf_op jit(solution)/shard_map/all_to_all | solution.py:81
  109.6 11.4 %copy.61 = bf16[128,128,256]{2,0,1:T(8,128)(2,1)} copy(bf16[128,128,256]{2,1,0:T(8,128)(2,1)} %bitcast.119) | data formatting | bytes 16777216 | tf_op jit(solution)/shard_map/all_to_all | solution.py:81
  121.0 167.7 %all-to-all-done.1 = bf16[128,128,256]{2,0,1:T(8,128)(2,1)} async-done(((bf16[128,128,256]{2,0,1:T(8,128)(2,1)}), bf16[128,128,256]{2,0,1:T(8,128)(2,1)}, u32[]{:S(2)}, u32[]{:S(2)}) %all-to-all-start.1) | async-done | bytes 8388640 | tf_op jit(solution)/shard_map/all_to_all | solution.py:73
  288.7 6.0 all-to-all-start.5
  294.8 4.0 gather_fusion.1
  298.8 0.0 copy-done.7
  298.8 9.6 multiply_convert_fusion
  308.4 4.0 gather_fusion.2
  312.4 0.0 copy-done
  312.5 0.6 gather_fusion
  313.1 0.1 broadcast_select_fusion.7
  313.2 0.2 broadcast_select_fusion.15
  313.3 12.5 %copy.49 = bf16[16,128,8,256]{3,2,1,0:T(8,128)(2,1)} copy(bf16[16,128,8,256]{3,1,2,0:T(8,128)(2,1)} %bitcast.10) | data formatting | bytes 16777216 | tf_op jit(solution)/shard_map/all_to_all | solution.py:73
  325.8 48.3 %fusion.22 = f32[8,256,1024]{2,1,0:T(8,128)} fusion(bf16[2048,8,256]{2,1,0:T(8,128)(2,1)} %bitcast.124, s32[1024]{0:T(1024)S(1)} %fusion.89, pred[1024]{0:T(1024)(128)(4,1)S(1)} %fusion.92, bf16[8,256,256]{2,1,0:T(8,128)(2,1)S(1)} %broadcast_select_fusion.15), kind=kOutput, calls=%fused_computation.43 | convolution fusion | flops 9701425152 | bytes 17830912 | tf_op jit(solution)/shard_map/kcr,crj->kcj/dot_general | solution.py:35
  374.1 4.5 fusion.52
  378.6 0.0 copy-start.2
  378.6 41.4 %convolution_convert_fusion.1 = bf16[2048,8,256]{2,0,1:T(8,128)(2,1)S(1)} fusion(f32[1024,8,256]{0,2,1:T(8,128)S(1)} %fusion.52, s32[1024]{0:T(1024)S(1)} %fusion.89, pred[1024]{0:T(1024)(128)(4,1)S(1)} %fusion.92), kind=kOutput, calls=%fused_computation.34 | convolution fusion | flops 8631877632 | bytes 16782336 | tf_op jit(solution)/shard_map/kz,kcr->zcr/dot_general | solution.py:105
  420.0 0.0 copy-done.2
  420.0 22.3 %copy.55 = bf16[2048,8,256]{2,1,0:T(8,128)(2,1)} copy(bf16[2048,8,256]{2,0,1:T(8,128)(2,1)S(1)} %convolution_convert_fusion.1) | data formatting | bytes 16777216 | tf_op jit(solution)/shard_map/convert_element_type | solution.py:107
  442.4 40.8 %all-to-all-done.5 = bf16[128,128,256]{2,0,1:T(8,128)(2,1)} async-done(((bf16[128,128,256]{2,0,1:T(8,128)(2,1)}), bf16[128,128,256]{2,0,1:T(8,128)(2,1)}, u32[]{:S(2)}, u32[]{:S(2)}) %all-to-all-start.5) | async-done | bytes 8388640 | tf_op jit(solution)/shard_map/all_to_all | solution.py:80
  483.1 5.8 all-to-all-start.2
  489.0 34.9 %fusion.182 = bf16[1024,2048,1]{0,1,2:T(8,128)(2,1)} fusion(s32[1024]{0:T(1024)S(1)} %fusion.89, pred[1024]{0:T(1024)(128)(4,1)S(1)} %fusion.92), kind=kLoop, calls=%fused_computation.35.clone.clone.1 | loop fusion | flops 35651584 | bytes 4199424 | tf_op jit(solution)/shard_map/kz,zcr->kcr/dot_general | solution.py:91
  523.9 9.3 copy.66
  533.1 12.5 %copy.63 = bf16[16,128,8,256]{3,2,1,0:T(8,128)(2,1)} copy(bf16[16,128,8,256]{3,1,2,0:T(8,128)(2,1)} %bitcast.29) | data formatting | bytes 16777216 | tf_op jit(solution)/shard_map/all_to_all | solution.py:80
  545.7 4.8 slice_multiply_fusion.1
  550.5 0.7 pad_maximum_fusion
  551.2 14.3 %fusion.7 = bf16[1024,8,256]{2,0,1:T(8,128)(2,1)} fusion(bf16[2048,8,256]{2,1,0:T(8,128)(2,1)} %bitcast.123, bf16[1024,2048,1]{0,1,2:T(8,128)(2,1)} %fusion.182), kind=kOutput, calls=%fused_computation.21 | convolution fusion | flops 8589934592 | bytes 16777216 | tf_op jit(solution)/shard_map/kz,zcr->kcr/dot_general | solution.py:91
  565.5 6.3 fusion.16
  571.8 2.7 fusion.185
  574.5 41.4 %convolution_convert_fusion = bf16[2048,8,256]{2,0,1:T(8,128)(2,1)S(1)} fusion(s32[1024]{0:T(1024)S(1)} %fusion.89, pred[1024]{0:T(1024)(128)(4,1)S(1)} %fusion.92, bf16[1024,8,256]{0,2,1:T(8,128)(2,1)S(1)} %fusion.185), kind=kOutput, calls=%fused_computation.33 | convolution fusion | flops 8629780480 | bytes 12588032 | tf_op jit(solution)/shard_map/kz,kcr->zcr/dot_general | solution.py:108
  615.9 22.5 %copy.71 = bf16[2048,8,256]{2,1,0:T(8,128)(2,1)} copy(bf16[2048,8,256]{2,0,1:T(8,128)(2,1)S(1)} %convolution_convert_fusion) | data formatting | bytes 16777216 | tf_op jit(solution)/shard_map/convert_element_type | solution.py:110
  638.4 34.7 %all-to-all-done.2 = bf16[2048,8,256]{2,1,0:T(8,128)(2,1)} async-done(((bf16[2048,8,256]{2,1,0:T(8,128)(2,1)}), bf16[2048,8,256]{2,1,0:T(8,128)(2,1)}, u32[]{:S(2)}, u32[]{:S(2)}) %all-to-all-start.2) | async-done | bytes 8388640 | tf_op jit(solution)/shard_map/all_to_all | solution.py:113
  673.1 7.9 copy.109
  681.0 21.6 %all_to_all.144 = bf16[128,128,256]{2,1,0:T(8,128)(2,1)} all-to-all(bf16[128,128,256]{2,1,0:T(8,128)(2,1)} %bitcast.120), channel_id=1, replica_groups=mesh['ax'=16,'az'=2] {'az'}, dimensions={0} | all-to-all | bytes 16777216 | tf_op jit(solution)/shard_map/all_to_all | solution.py:112
  702.6 5.5 all-to-all-start.6
  708.1 21.1 %copy.57 = bf16[64,2,128,256]{2,1,3,0:T(2,128)(2,1)} copy(bf16[64,2,128,256]{3,2,0,1:T(8,128)(2,1)} %bitcast.117) | data formatting | bytes 16777216 | tf_op jit(solution)/shard_map/all_to_all | solution.py:112
  729.1 14.1 %all_to_all.119 = bf16[64,256,256]{1,2,0:T(8,128)(2,1)} reshape(bf16[64,2,128,256]{2,1,3,0:T(2,128)(2,1)} %copy.57) | data formatting | bytes 16777216 | tf_op jit(solution)/shard_map/all_to_all | solution.py:112
  743.2 155.0 %all-to-all-done.6 = bf16[2048,8,256]{2,1,0:T(8,128)(2,1)} async-done(((bf16[2048,8,256]{2,1,0:T(8,128)(2,1)}), bf16[2048,8,256]{2,1,0:T(8,128)(2,1)}, u32[]{:S(2)}, u32[]{:S(2)}) %all-to-all-start.6) | async-done | bytes 8388640 | tf_op jit(solution)/shard_map/all_to_all | solution.py:120
  898.2 7.9 copy.108
  906.1 19.8 %all_to_all.145 = bf16[128,128,256]{2,1,0:T(8,128)(2,1)} all-to-all(bf16[128,128,256]{2,1,0:T(8,128)(2,1)} %bitcast.121), channel_id=1, replica_groups=mesh['ax'=16,'az'=2] {'az'}, dimensions={0} | all-to-all | bytes 16777216 | tf_op jit(solution)/shard_map/all_to_all | solution.py:119
  926.0 21.1 %copy.73 = bf16[64,2,128,256]{2,1,3,0:T(2,128)(2,1)} copy(bf16[64,2,128,256]{3,2,0,1:T(8,128)(2,1)} %bitcast.122) | data formatting | bytes 16777216 | tf_op jit(solution)/shard_map/all_to_all | solution.py:119
  947.0 14.1 %all_to_all.135 = bf16[64,256,256]{1,2,0:T(8,128)(2,1)} reshape(bf16[64,2,128,256]{2,1,3,0:T(2,128)(2,1)} %copy.73) | data formatting | bytes 16777216 | tf_op jit(solution)/shard_map/all_to_all | solution.py:119
  961.1 0.0 copy-done.4
  961.1 0.0 copy-done.6
  961.1 13.7 %convert_bitcast_fusion = bf16[64,512,256]{1,2,0:T(8,128)(2,1)} fusion(bf16[64,256,256]{1,2,0:T(8,128)(2,1)} %all_to_all.135, s32[256]{0:T(256)S(1)} %copy-done.4, pred[256]{0:T(512)(128)(4,1)S(1)} %copy-done.6), kind=kOutput, calls=%fused_computation.3 | convolution fusion | flops 4305584128 | bytes 25167104 | tf_op jit(solution)/shard_map/ct,zcr->ztr/dot_general | solution.py:130
  974.8 22.4 %copy.75 = bf16[64,512,256]{2,1,0:T(8,128)(2,1)} copy(bf16[64,512,256]{1,2,0:T(8,128)(2,1)} %convert_bitcast_fusion) | data formatting | bytes 33554432
  997.2 13.7 %convert_bitcast_fusion.1 = bf16[64,512,256]{1,2,0:T(8,128)(2,1)} fusion(bf16[64,256,256]{1,2,0:T(8,128)(2,1)} %all_to_all.119, s32[256]{0:T(256)S(1)} %copy-done.4, pred[256]{0:T(512)(128)(4,1)S(1)} %copy-done.6), kind=kOutput, calls=%fused_computation.4 | convolution fusion | flops 4305584128 | bytes 25167104 | tf_op jit(solution)/shard_map/ct,zcr->ztr/dot_general | solution.py:127
  1010.8 22.4 %copy.74 = bf16[64,512,256]{2,1,0:T(8,128)(2,1)} copy(bf16[64,512,256]{1,2,0:T(8,128)(2,1)} %convert_bitcast_fusion.1) | data formatting | bytes 33554432
  (20 shorter events, 0.1 us)
Async XLA Ops:
  0.6 311.8 %copy-start = (f32[64,256]{1,0:T(8,128)S(1)}, f32[64,256]{1,0:T(8,128)}, u32[]{:S(2)}) copy-start(f32[64,256]{1,0:T(8,128)} %param.10) | copy-start | bytes 196612
  0.7 34.3 %copy-start.5 = (pred[256]{0:T(512)(128)(4,1)}, pred[256]{0:T(512)(128)(4,1)S(1)}, u32[]{:S(2)}) copy-start(pred[256]{0:T(512)(128)(4,1)S(1)} %compare_and_fusion.1) | copy-start | bytes 772
  0.7 34.3 %copy-start.3 = (s32[256]{0:T(256)}, s32[256]{0:T(256)S(1)}, u32[]{:S(2)}) copy-start(s32[256]{0:T(256)S(1)} %fusion.93) | copy-start | bytes 3076
  26.9 34.2 %all-to-all-start = ((bf16[64,256,256]{2,0,1:T(8,128)(2,1)}), bf16[64,256,256]{2,0,1:T(8,128)(2,1)}, u32[]{:S(2)}, u32[]{:S(2)}) async-start(bf16[64,256,256]{2,0,1:T(8,128)(2,1)} %copy.44), calls=%async_computation | async-start | bytes 16777216 | tf_op jit(solution)/shard_map/all_to_all | solution.py:74
  61.0 30.3 %all-to-all-start.4 = ((bf16[64,256,256]{2,0,1:T(8,128)(2,1)}), bf16[64,256,256]{2,0,1:T(8,128)(2,1)}, u32[]{:S(2)}, u32[]{:S(2)}) async-start(bf16[64,256,256]{2,0,1:T(8,128)(2,1)} %copy.58), calls=%async_computation.4 | async-start | bytes 16777216 | tf_op jit(solution)/shard_map/all_to_all | solution.py:81
  91.3 197.4 %all-to-all-start.1 = ((bf16[128,128,256]{2,0,1:T(8,128)(2,1)}), bf16[128,128,256]{2,0,1:T(8,128)(2,1)}, u32[]{:S(2)}, u32[]{:S(2)}) async-start(bf16[128,128,256]{2,0,1:T(8,128)(2,1)} %copy.47), calls=%async_computation.1 | async-start | bytes 16777216 | tf_op jit(solution)/shard_map/all_to_all | solution.py:73
  121.0 177.7 %copy-start.7 = (f32[256]{0:T(256)S(1)}, f32[256]{0:T(256)}, u32[]{:S(2)}) copy-start(f32[256]{0:T(256)} %param.11) | copy-start | bytes 3076
  288.7 194.4 %all-to-all-start.5 = ((bf16[128,128,256]{2,0,1:T(8,128)(2,1)}), bf16[128,128,256]{2,0,1:T(8,128)(2,1)}, u32[]{:S(2)}, u32[]{:S(2)}) async-start(bf16[128,128,256]{2,0,1:T(8,128)(2,1)} %copy.61), calls=%async_computation.5 | async-start | bytes 16777216 | tf_op jit(solution)/shard_map/all_to_all | solution.py:80
  378.6 41.5 %copy-start.2 = (f32[1024,8,256]{0,2,1:T(8,128)}, f32[1024,8,256]{0,2,1:T(8,128)S(1)}, u32[]{:S(2)}) copy-start(f32[1024,8,256]{0,2,1:T(8,128)S(1)} %fusion.52) | copy-start | bytes 25165828
  483.1 190.0 %all-to-all-start.2 = ((bf16[2048,8,256]{2,1,0:T(8,128)(2,1)}), bf16[2048,8,256]{2,1,0:T(8,128)(2,1)}, u32[]{:S(2)}, u32[]{:S(2)}) async-start(bf16[2048,8,256]{2,1,0:T(8,128)(2,1)} %copy.55), calls=%async_computation.2 | async-start | bytes 16777216 | tf_op jit(solution)/shard_map/all_to_all | solution.py:113
  702.6 195.6 %all-to-all-start.6 = ((bf16[2048,8,256]{2,1,0:T(8,128)(2,1)}), bf16[2048,8,256]{2,1,0:T(8,128)(2,1)}, u32[]{:S(2)}, u32[]{:S(2)}) async-start(bf16[2048,8,256]{2,1,0:T(8,128)(2,1)} %copy.71), calls=%async_computation.6 | async-start | bytes 16777216 | tf_op jit(solution)/shard_map/all_to_all | solution.py:120
  947.0 14.1 %copy-start.4 = (s32[256]{0:T(256)S(1)}, s32[256]{0:T(256)}, u32[]{:S(2)}) copy-start(s32[256]{0:T(256)} %copy-done.3) | copy-start | bytes 3076
  947.0 14.1 %copy-start.6 = (pred[256]{0:T(512)(128)(4,1)S(1)}, pred[256]{0:T(512)(128)(4,1)}, u32[]{:S(2)}) copy-start(pred[256]{0:T(512)(128)(4,1)} %copy-done.5) | copy-start | bytes 772
  1010.8 22.4 %copy-start.1 = (f32[64,256]{1,0:T(8,128)S(1)}, f32[64,256]{1,0:T(8,128)}, u32[]{:S(2)}) copy-start(f32[64,256]{1,0:T(8,128)} %param.10) | copy-start | bytes 196612
where the time goes:
time: 1040 us; the launch traced here: 1030 us
  waiting for transfers between devices  398 us (38%)
  local copies, waits for them, and re-layouts  288 us (28%)
  matrix products  216 us (21%)
  other arithmetic  50.4 us (5%)
  blocking collectives  41.4 us (4%)
  starting transfers between devices  39.2 us (4%)
    all_to_all x1, waiting for transfers between devices, per_device(): lax.all_to_all(lax.all_to_all(source_coef, 'az', split_axis=1, concat_axi...  168 us
    all_to_all x1, waiting for transfers between devices, per_device(): lax.all_to_all(velocity_cols, 'ax', split_axis=0, concat_axis=1, tiled=True)  155 us
    dot_general x1, matrix products, radial_solve(): jnp.einsum('kcr,crj->kcj', source_hat, weighted_rows, preferred_element_t...  48.3 us
    unnamed x18, local copies, waits for them, and re-layouts  44.8 us
    dot_general x1, matrix products, per_device(): jnp.einsum('kz,kcr->zcr', axial_table, velocity_hat, preferred_element_ty...  41.4 us
    dot_general x1, matrix products, per_device(): jnp.einsum('kz,kcr->zcr', axial_table, pressure_hat, preferred_element_ty...  41.4 us
    all_to_all x1, waiting for transfers between devices, per_device(): lax.all_to_all(lax.all_to_all(forcing_coef, 'az', split_axis=1, concat_ax...  40.8 us
    all_to_all x2, local copies, waits for them, and re-layouts, per_device(): lax.all_to_all(lax.all_to_all(pressure_cols, 'ax', split_axis=0, concat_a...  35.2 us
  transfers between devices with their start and end apart: 6, of which 4 were waited for; matrix products, arithmetic and copies ran while one was open for 38% of the time, Pallas kernels for 0%

commit v1 on v0

v1 whole, which is shorter than its diff:
```python
import functools
import math

import jax
import jax.numpy as jnp
from jax import lax
from jax.experimental import pallas as pl
from jax.experimental.layout import Layout, with_layout_constraint
from jax.experimental.pallas import tpu as pltpu
from jax.sharding import PartitionSpec as P

VISCOUS = 0.5
LENGTH = 8.0


def fourier_table(coef_count, point_count):
    slot_index = jnp.arange(coef_count, dtype=jnp.int32)
    frequency = jnp.where(slot_index == 1, coef_count // 2, slot_index // 2)
    sine_row = (slot_index % 2 == 1) & (slot_index != 1)
    grid_points = jnp.arange(point_count, dtype=jnp.int32)
    phase_index = frequency[:, None] * grid_points[None, :] % point_count
    angles = phase_index.astype(jnp.float32) * (2.0 * math.pi / point_count)
    table_values = jnp.where(sine_row[:, None], jnp.sin(angles), jnp.cos(angles)) * math.sqrt(
        2.0 / point_count
    )
    return table_values.astype(jnp.bfloat16)


def plane_block(plane_count):
    return 8 if plane_count % 8 == 0 else 1


def coef_kernel(ax_count, az_count, coef_local, table_ref, plane_ref, out_ref):
    planes, _, radial = plane_ref.shape
    half = ax_count * coef_local
    for z in range(planes):
        coefs = jnp.dot(table_ref[...], plane_ref[z], preferred_element_type=jnp.float32)
        for part in range(az_count):
            rows = coefs[part * half : (part + 1) * half]
            out_ref[:, part, z] = rows.reshape(ax_count, coef_local, radial).astype(out_ref.dtype)


def to_coef(table, planes, ax_count, az_count):
    coef_count, point_count = table.shape
    plane_count, _, radial = planes.shape
    coef_local = coef_count // (ax_count * az_count)
    block = plane_block(plane_count)
    return pl.pallas_call(
        functools.partial(coef_kernel, ax_count, az_count, coef_local),
        grid=(plane_count // block,),
        in_specs=[
            pl.BlockSpec((coef_count, point_count), lambda i: (0, 0)),
            pl.BlockSpec((block, point_count, radial), lambda i: (i, 0, 0)),
        ],
        out_specs=pl.BlockSpec(
            (ax_count, az_count, block, coef_local, radial), lambda i: (0, 0, i, 0, 0)
        ),
        out_shape=jax.ShapeDtypeStruct(
            (ax_count, az_count, plane_count, coef_local, radial), jnp.bfloat16
        ),
        cost_estimate=pl.CostEstimate(
            flops=2 * plane_count * coef_count * point_count * radial,
            bytes_accessed=2 * plane_count * (coef_count + point_count) * radial,
            transcendentals=0,
        ),
        compiler_params=pltpu.CompilerParams(vmem_limit_bytes=56 * 2**20),
        name="to_coef",
    )(table, planes)


def grid_kernel(ax_count, az_count, coef_local, table_ref, coef_ref, out_ref):
    planes, _, radial = out_ref.shape
    half = ax_count * coef_local
    for z in range(planes):
        parts = [
            coef_ref[:, part, z].astype(jnp.float32).reshape(half, radial)
            for part in range(az_count)
        ]
        coefs = jnp.concatenate(parts, axis=0).astype(jnp.bfloat16)
        out_ref[z] = jnp.dot(
            table_ref[...], coefs, preferred_element_type=jnp.float32
        ).astype(out_ref.dtype)


def to_grid(table_t, coefs):
    point_count, coef_count = table_t.shape
    ax_count, az_count, plane_count, coef_local, radial = coefs.shape
    block = plane_block(plane_count)
    return pl.pallas_call(
        functools.partial(grid_kernel, ax_count, az_count, coef_local),
        grid=(plane_count // block,),
        in_specs=[
            pl.BlockSpec((point_count, coef_count), lambda i: (0, 0)),
            pl.BlockSpec(
                (ax_count, az_count, block, coef_local, radial), lambda i: (0, 0, i, 0, 0)
            ),
        ],
        out_specs=pl.BlockSpec((block, point_count, radial), lambda i: (i, 0, 0)),
        out_shape=jax.ShapeDtypeStruct((plane_count, point_count, radial), jnp.bfloat16),
        cost_estimate=pl.CostEstimate(
            flops=2 * plane_count * coef_count * point_count * radial,
            bytes_accessed=2 * plane_count * (coef_count + point_count) * radial,
            transcendentals=0,
        ),
        compiler_params=pltpu.CompilerParams(vmem_limit_bytes=56 * 2**20),
        name="to_grid",
    )(table_t, coefs)


def per_device(source, forcing, radial_basis, eigenvalues, radial_weight):
    ax_count = lax.axis_size("ax")
    az_count = lax.axis_size("az")
    device_count = ax_count * az_count
    plane_local, point_count, radial = source.shape
    plane_count = plane_local * device_count
    coef_count = 2 * radial_basis.shape[0] * az_count
    wave_count = plane_count // 2
    coef_local = coef_count // device_count
    az_table = fourier_table(coef_count, point_count)

    def exchange(blocks):
        flat = blocks.reshape(device_count, plane_local, coef_local, radial)
        return lax.all_to_all(flat, ("ax", "az"), split_axis=0, concat_axis=0, tiled=True)

    def to_owner(planes):
        received = exchange(to_coef(az_table, planes, ax_count, az_count))
        return received.reshape(plane_count, coef_local, radial)

    def to_planes(cols):
        received = exchange(cols)
        blocks = received.reshape(ax_count, az_count, plane_local, coef_local, radial)
        return to_grid(az_table.T, blocks)

    source_blocks = to_coef(az_table, source, ax_count, az_count)
    source_cols = exchange(source_blocks).reshape(plane_count, coef_local, radial)
    forcing_cols = to_owner(forcing)
    axial_table = lax.optimization_barrier(fourier_table(wave_count, plane_count))

    first_coef = lax.axis_index("ax") * coef_local
    pair_index = (first_coef + jnp.arange(coef_local, dtype=jnp.int32)) // 2
    basis_rows = jnp.take(radial_basis, pair_index, axis=0)
    eigen_rows = jnp.take(eigenvalues, pair_index, axis=0)[:, None, :]
    weighted_rows = (radial_weight[None, :, None] * basis_rows.astype(jnp.float32)).astype(
        jnp.bfloat16
    )
    wave_index = jnp.arange(wave_count, dtype=jnp.int32)
    wavenumber = (wave_index // 2).astype(jnp.float32) * (LENGTH / wave_count)
    wave_sq = (wavenumber * wavenumber)[None, :, None]

    def axial(cols):
        return jnp.einsum(
            "kz,zcr->kcr", axial_table, cols, preferred_element_type=jnp.float32
        ).astype(jnp.bfloat16).transpose(1, 0, 2)

    def axial_back(hat):
        return jnp.einsum(
            "kz,ckr->zcr", axial_table, hat, preferred_element_type=jnp.float32
        ).astype(jnp.bfloat16)

    def transform(hat):
        return jnp.einsum(
            "ckr,crj->ckj", hat, weighted_rows, preferred_element_type=jnp.float32
        )

    def back(scaled):
        return jnp.einsum(
            "ckj,crj->ckr", scaled, basis_rows, preferred_element_type=jnp.float32
        )

    scaled = (transform(axial(source_cols)) / (eigen_rows + wave_sq)).astype(jnp.bfloat16)
    pressure_full = back(scaled)
    pressure_cols = with_layout_constraint(
        axial_back(pressure_full.astype(jnp.bfloat16)), Layout(major_to_minor=(0, 1, 2))
    )
    pressure_blocks, forcing_cols = lax.optimization_barrier((pressure_cols, forcing_cols))
    pressure = to_planes(pressure_blocks)

    paired = pressure_full.reshape(coef_local, wave_count // 2, 2, radial)
    pair_wave = wavenumber.reshape(wave_count // 2, 2)[:, 0][None, :, None]
    gradient = jnp.stack(
        [pair_wave * paired[:, :, 1], -pair_wave * paired[:, :, 0]], axis=2
    ).reshape(pressure_full.shape)
    helm_rhs = (axial(forcing_cols).astype(jnp.float32) - gradient).astype(jnp.bfloat16)
    scaled_visc = (
        transform(helm_rhs) / (1.0 + VISCOUS * (eigen_rows + wave_sq))
    ).astype(jnp.bfloat16)
    velocity = to_planes(axial_back(back(scaled_visc).astype(jnp.bfloat16)))
    return (pressure, velocity)


def solution(mesh):
    placed = (
        P(("ax", "az"), None, None),
        P(("ax", "az"), None, None),
        P("az", None, None),
        P("az", None),
        P(),
    )
    return jax.shard_map(
        per_device,
        mesh=mesh,
        in_specs=placed,
        out_specs=(P(("ax", "az"), None, None), P(("ax", "az"), None, None)),
        check_vma=False,
    )
```

time: 1040 us -> 802 us (0.77)
  local copies, waits for them, and re-layouts: 288 us -> 69.6 us
  matrix products: 216 us -> 68.9 us
  waiting for transfers between devices: 398 us -> 504 us
  Pallas kernels: 0 us -> 52 us
  blocking collectives: 41.4 us -> 0 us
  other arithmetic: 50.4 us -> 60.9 us
    all_to_all x12 -> x0, local copies, waits for them, and re-layouts: 157 us -> none  [the longest x2 35.2 us: per_device(): lax.all_to_all(lax.all_to_all(pressure_cols, 'ax', split_axis=0, concat_a...]
    dot_general x11 -> x5, matrix products: 216 us -> 68.9 us  [the longest x2 29.1 us: axial_back(): jnp.einsum('kz,ckr->zcr', axial_table, hat, preferred_element_type=jnp.fl...]
    all_to_all x6 -> x4, waiting for transfers between devices: 398 us -> 504 us  [exchange(): lax.all_to_all(flat, ('ax', 'az'), split_axis=0, concat_axis=0, tiled=True)]
    convert_element_type x4 -> x0, local copies, waits for them, and re-layouts: 67.8 us -> none  [the longest x1 22.5 us: per_device(): velocity_cols = jnp.einsum('kz,kcr->zcr', axial_table, velocity_hat, pref...]
    pallas_call x0 -> x4, Pallas kernels: none -> 52 us  [the longest x2 26.5 us: to_coef(): pl.pallas_call(functools.partial(coef_kernel, ax_count, az_count, coef_lo...]
    unnamed x18 -> x16, local copies, waits for them, and re-layouts: 44.8 us -> 1.12 us
    all_to_all x2 -> x0, blocking collectives: 41.4 us -> none  [the longest x1 21.6 us: per_device(): lax.all_to_all(lax.all_to_all(pressure_cols, 'ax', split_axis=0, concat_a...]
    reshape x0 -> x3, local copies, waits for them, and re-layouts: none -> 36.9 us  [the longest x1 15.4 us: exchange(): flat = blocks.reshape(device_count, plane_local, coef_local, radial)]
  transfers between devices with their start and end apart: 6 -> 4, of which waited for: 4 -> 4; matrix products, arithmetic and copies ran while one was open for 38% -> 25% of each run, Pallas kernels for 0% -> 3%
where the time goes in v1:
time: 802 us; the launch traced here: 788 us
  waiting for transfers between devices  504 us (63%)
  local copies, waits for them, and re-layouts  69.6 us (9%)
  matrix products  68.9 us (9%)
  other arithmetic  60.9 us (8%)
  Pallas kernels  52 us (6%)
  starting transfers between devices  31.9 us (4%)
    all_to_all x4, waiting for transfers between devices, exchange(): lax.all_to_all(flat, ('ax', 'az'), split_axis=0, concat_axis=0, tiled=True)  504 us
    convert_element_type x3, other arithmetic, fourier_table(): return table_values.astype(jnp.bfloat16)  40.2 us
    all_to_all x4, starting transfers between devices, exchange(): lax.all_to_all(flat, ('ax', 'az'), split_axis=0, concat_axis=0, tiled=True)  31.9 us
    dot_general x2, matrix products, axial_back(): jnp.einsum('kz,ckr->zcr', axial_table, hat, preferred_element_type=jnp.fl...  29.1 us
    pallas_call x2, Pallas kernels, to_coef(): pl.pallas_call(functools.partial(coef_kernel, ax_count, az_count, coef_lo...  26.5 us
    pallas_call x2, Pallas kernels, to_grid(): pl.pallas_call(functools.partial(grid_kernel, ax_count, az_count, coef_lo...  25.5 us
    dot_general x1, local copies, waits for them, and re-layouts, axial_back(): jnp.einsum('kz,ckr->zcr', axial_table, hat, preferred_element_type=jnp.fl...  22.6 us
    dot_general x1, matrix products, transform(): jnp.einsum('ckr,crj->ckj', hat, weighted_rows, preferred_element_type=jnp...  18 us
  transfers between devices with their start and end apart: 4, of which 4 were waited for; matrix products, arithmetic and copies ran while one was open for 25% of the time, Pallas kernels for 3%

profile of v1, /device:TPU:29, one launch (start us, length us, event | category | flops | bytes accessed | tf_op | source)
XLA Modules:
  0.0 788.1 jit_solution(6891675768382733326)
XLA Ops:
  0.6 0.0 copy-start
  0.7 0.0 copy-start.5
  0.7 0.5 copy-done.5
  1.2 0.0 copy-start.3
  1.2 0.6 copy-done.3
  1.8 3.1 multiply_convert_fusion.5.table_ref
  4.9 13.2 %to_coef.2 = bf16[16,2,64,8,256]{4,3,2,1,0:T(8,128)(2,1)} custom-call(bf16[256,512]{1,0:T(8,128)(2,1)} %multiply_convert_fusion.5.table_ref, bf16[64,512,256]{2,1,0:T(8,128)(2,1)} %plane_ref.2), custom_call_target="tpu_custom_call" | custom-call | flops 4294967296 | bytes 25165824 | tf_op jit(solution)/shard_map/to_coef/pallas_call | solution.py:48
  18.1 6.2 all-to-all-start
  24.3 13.3 %to_coef.3 = bf16[16,2,64,8,256]{4,3,2,1,0:T(8,128)(2,1)} custom-call(bf16[256,512]{1,0:T(8,128)(2,1)} %multiply_convert_fusion.5.table_ref, bf16[64,512,256]{2,1,0:T(8,128)(2,1)} %plane_ref.3), custom_call_target="tpu_custom_call" | custom-call | flops 4294967296 | bytes 25165824 | tf_op jit(solution)/shard_map/to_coef/pallas_call | solution.py:48
  37.6 168.1 %all-to-all-done = bf16[32,64,8,256]{3,2,1,0:T(8,128)(2,1)} async-done(((bf16[32,64,8,256]{3,2,1,0:T(8,128)(2,1)}), bf16[32,64,8,256]{3,2,1,0:T(8,128)(2,1)}, u32[]{:S(2)}, u32[]{:S(2)}) %all-to-all-start) | async-done | bytes 8388640 | tf_op jit(solution)/shard_map/all_to_all | solution.py:123
  205.7 8.2 %all-to-all-start.1 = ((bf16[32,64,8,256]{3,2,1,0:T(8,128)(2,1)}), bf16[32,64,8,256]{3,2,1,0:T(8,128)(2,1)}, u32[]{:S(2)}, u32[]{:S(2)}) async-start(bf16[32,64,8,256]{3,2,1,0:T(8,128)(2,1)} %bitcast.32), calls=%async_computation.1 | async-start | bytes 16777216 | tf_op jit(solution)/shard_map/all_to_all | solution.py:123
  214.0 0.0 copy-done
  214.0 0.6 gather_fusion.1
  214.5 4.0 gather_fusion
  218.6 34.1 %multiply_convert_fusion = bf16[1024,2048]{0,1:T(8,128)(2,1)S(1)} fusion(s32[1024]{0:T(1024)S(1)} %fusion.70, pred[1024]{0:T(1024)(128)(4,1)S(1)} %fusion.73), kind=kLoop, calls=%fused_computation.22 | loop fusion | flops 35651584 | bytes 4199424 | tf_op jit(solution)/shard_map/convert_element_type | solution.py:26
  252.7 0.0 copy-start.7
  252.7 0.1 broadcast_select_fusion.1
  252.8 13.3 %fusion.9 = bf16[1024,8,256]{2,0,1:T(8,128)(2,1)S(1)} fusion(bf16[2048,8,256]{2,1,0:T(8,128)(2,1)} %bitcast.2, bf16[1024,2048]{0,1:T(8,128)(2,1)S(1)} %multiply_convert_fusion), kind=kOutput, calls=%fused_computation.20 | convolution fusion | flops 8589934592 | bytes 16777216 | tf_op jit(solution)/shard_map/kz,zcr->kcr/dot_general | solution.py:151
  266.1 0.0 copy-done.7
  266.1 0.0 copy-start.2
  266.2 4.4 copy.34
  270.6 0.0 copy-done.2
  270.6 8.5 %fusion.30 = f32[8,1024,256]{2,1,0:T(8,128)} fusion(f32[1024]{0:T(1024)S(1)} %fusion.72, f32[8,256]{1,0:T(8,128)S(1)} %broadcast_select_fusion.1, bf16[8,1024,256]{2,0,1:T(8,128)(2,1)} %bitcast.36, f32[256]{0:T(256)S(1)} %copy-done.2, bf16[8,256,256]{2,1,0:T(8,128)(2,1)S(1)} %gather_fusion, pred[8]{0:T(512)(128)(4,1)S(1)} %compare_and_fusion), kind=kOutput, calls=%fused_computation.43 | convolution fusion | flops 2156396544 | bytes 13644808 | tf_op jit(solution)/shard_map/ckj,crj->ckr/dot_general | solution.py:166
  279.1 12.6 %fusion.20 = bf16[2048,8,256]{2,0,1:T(8,128)(2,1)S(1)} fusion(bf16[1024,2048]{0,1:T(8,128)(2,1)} %copy-done.7, f32[8,1024,256]{2,1,0:T(8,128)} %fusion.30), kind=kOutput, calls=%fused_computation.34 | convolution fusion | flops 8592031744 | bytes 20971520 | tf_op jit(solution)/shard_map/kz,ckr->zcr/dot_general | solution.py:156
  291.7 22.6 %copy.33 = bf16[2048,8,256]{2,1,0:T(8,128)(2,1)} copy(bf16[2048,8,256]{2,0,1:T(8,128)(2,1)S(1)} %fusion.20) | data formatting | bytes 16777216 | tf_op jit(solution)/shard_map/kz,ckr->zcr/dot_general | solution.py:156
  314.3 80.9 %all-to-all-done.1 = bf16[32,64,8,256]{3,2,1,0:T(8,128)(2,1)} async-done(((bf16[32,64,8,256]{3,2,1,0:T(8,128)(2,1)}), bf16[32,64,8,256]{3,2,1,0:T(8,128)(2,1)}, u32[]{:S(2)}, u32[]{:S(2)}) %all-to-all-start.1) | async-done | bytes 8388640 | tf_op jit(solution)/shard_map/all_to_all | solution.py:123
  395.2 9.1 %all-to-all-start.2 = ((bf16[32,64,8,256]{3,2,1,0:T(8,128)(2,1)}), bf16[32,64,8,256]{3,2,1,0:T(8,128)(2,1)}, u32[]{:S(2)}, u32[]{:S(2)}) async-start(bf16[32,64,8,256]{3,2,1,0:T(8,128)(2,1)} %bitcast.34), calls=%async_computation.2 | async-start | bytes 16777216 | tf_op jit(solution)/shard_map/all_to_all | solution.py:123
  404.4 10.6 %reshape.209 = f32[8,512,2,256]{3,2,1,0:T(2,128)} reshape(f32[8,1024,256]{2,1,0:T(8,128)} %fusion.30) | data formatting | bytes 16777216 | tf_op jit(solution)/shard_map/reshape | solution.py:178
  415.0 11.9 %slice_multiply_fusion.1 = (f32[8,512,1,256]{3,2,1,0:T(1,128)S(1)}, f32[8,512,1,256]{3,2,1,0:T(1,128)S(1)}) fusion(f32[8,512,2,256]{3,2,1,0:T(2,128)} %reshape.209, f32[512]{0:T(512)S(1)} %bitcast.38, f32[512]{0:T(512)S(1)} %neg.8), kind=kLoop, calls=%fused_computation.31 | loop fusion | flops 2097152 | bytes 16781312 | tf_op jit(solution)/shard_map/mul | solution.py:181
  426.9 8.7 %pad_maximum_fusion = f32[8,512,2,256]{3,2,1,0:T(2,128)} fusion(f32[8,512,1,256]{3,2,1,0:T(1,128)S(1)} %get-tuple-element.7, f32[8,512,1,256]{3,2,1,0:T(1,128)S(1)} %get-tuple-element.6), kind=kLoop, calls=%fused_computation.14 | loop fusion | flops 2097152 | bytes 16777216 | tf_op jit(solution)/shard_map/stack | solution.py:180
  435.6 10.9 %reshape.210 = f32[8,1024,256]{2,1,0:T(8,128)} reshape(f32[8,512,2,256]{3,2,1,0:T(2,128)} %pad_maximum_fusion) | data formatting | bytes 16777216 | tf_op jit(solution)/shard_map/reshape | solution.py:182
  446.5 18.0 %fusion.16 = f32[8,1024,256]{2,1,0:T(8,128)} fusion(f32[8,1024,256]{2,1,0:T(8,128)} %reshape.210, bf16[2048,8,256]{2,1,0:T(8,128)(2,1)} %bitcast.6, bf16[1024,2048]{0,1:T(8,128)(2,1)} %copy-done.7, f32[256]{0:T(256)S(1)} %copy-done.2, bf16[8,256,256]{2,1,0:T(8,128)(2,1)S(1)} %gather_fusion, pred[8]{0:T(512)(128)(4,1)S(1)} %compare_and_fusion), kind=kOutput, calls=%fused_computation.29 | convolution fusion | flops 9674162176 | bytes 30409736 | tf_op jit(solution)/shard_map/ckr,crj->ckj/dot_general | solution.py:161
  464.5 16.5 %convolution_convert_fusion = bf16[2048,8,256]{2,0,1:T(8,128)(2,1)} fusion(bf16[1024,2048]{0,1:T(8,128)(2,1)} %copy-done.7, f32[8,1024,256]{2,1,0:T(8,128)} %fusion.16, f32[1024]{0:T(1024)S(1)} %fusion.72, f32[8,256]{1,0:T(8,128)S(1)} %broadcast_select_fusion.1, bf16[8,256,256]{2,1,0:T(8,128)(2,1)S(1)} %gather_fusion, pred[8]{0:T(512)(128)(4,1)S(1)} %compare_and_fusion), kind=kOutput, calls=%fused_computation.27 | convolution fusion | flops 9680977920 | bytes 22032392 | tf_op jit(solution)/shard_map/kz,ckr->zcr/dot_general | solution.py:156
  481.1 15.4 %copy.10 = bf16[32,64,8,256]{3,2,1,0:T(8,128)(2,1)} copy(bf16[32,64,8,256]{3,1,0,2:T(8,128)(2,1)} %bitcast.35) | data formatting | bytes 16777216 | tf_op jit(solution)/shard_map/reshape | solution.py:122
  496.5 0.0 copy-start.4
  496.5 0.0 copy-start.6
  496.5 88.9 %all-to-all-done.2 = bf16[32,64,8,256]{3,2,1,0:T(8,128)(2,1)} async-done(((bf16[32,64,8,256]{3,2,1,0:T(8,128)(2,1)}), bf16[32,64,8,256]{3,2,1,0:T(8,128)(2,1)}, u32[]{:S(2)}, u32[]{:S(2)}) %all-to-all-start.2) | async-done | bytes 8388640 | tf_op jit(solution)/shard_map/all_to_all | solution.py:123
  585.4 8.4 %all-to-all-start.3 = ((bf16[32,64,8,256]{3,2,1,0:T(8,128)(2,1)}), bf16[32,64,8,256]{3,2,1,0:T(8,128)(2,1)}, u32[]{:S(2)}, u32[]{:S(2)}) async-start(bf16[32,64,8,256]{3,2,1,0:T(8,128)(2,1)} %copy.10), calls=%async_computation.3 | async-start | bytes 16777216 | tf_op jit(solution)/shard_map/all_to_all | solution.py:123
  593.8 0.0 copy-done.4
  593.8 0.0 copy-done.6
  593.9 2.9 multiply_convert_fusion.6.table_ref
  596.8 12.7 %to_grid.2 = bf16[64,512,256]{2,1,0:T(8,128)(2,1)} custom-call(bf16[512,256]{1,0:T(8,128)(2,1)} %multiply_convert_fusion.6.table_ref, bf16[16,2,64,8,256]{4,3,2,1,0:T(8,128)(2,1)} %bitcast.8.coef_ref), custom_call_target="tpu_custom_call" | custom-call | flops 4294967296 | bytes 25165824 | tf_op jit(solution)/shard_map/to_grid/pallas_call | solution.py:89
  609.5 165.6 %all-to-all-done.3 = bf16[32,64,8,256]{3,2,1,0:T(8,128)(2,1)} async-done(((bf16[32,64,8,256]{3,2,1,0:T(8,128)(2,1)}), bf16[32,64,8,256]{3,2,1,0:T(8,128)(2,1)}, u32[]{:S(2)}, u32[]{:S(2)}) %all-to-all-start.3) | async-done | bytes 8388640 | tf_op jit(solution)/shard_map/all_to_all | solution.py:123
  775.1 0.0 copy-start.1
  775.1 12.7 %to_grid.3 = bf16[64,512,256]{2,1,0:T(8,128)(2,1)} custom-call(bf16[512,256]{1,0:T(8,128)(2,1)} %multiply_convert_fusion.6.table_ref, bf16[16,2,64,8,256]{4,3,2,1,0:T(8,128)(2,1)} %bitcast.12.coef_ref), custom_call_target="tpu_custom_call" | custom-call | flops 4294967296 | bytes 25165824 | tf_op jit(solution)/shard_map/to_grid/pallas_call | solution.py:89
  787.9 0.0 copy-done.1
  (13 shorter events, 0.1 us)
Async XLA Ops:
  0.6 213.3 %copy-start = (f32[64,256]{1,0:T(8,128)S(1)}, f32[64,256]{1,0:T(8,128)}, u32[]{:S(2)}) copy-start(f32[64,256]{1,0:T(8,128)} %param.8) | copy-start | bytes 196612
  0.7 0.5 copy-start.5
  1.2 0.6 copy-start.3
  18.1 187.6 %all-to-all-start = ((bf16[32,64,8,256]{3,2,1,0:T(8,128)(2,1)}), bf16[32,64,8,256]{3,2,1,0:T(8,128)(2,1)}, u32[]{:S(2)}, u32[]{:S(2)}) async-start(bf16[32,64,8,256]{3,2,1,0:T(8,128)(2,1)} %bitcast.33), calls=%async_computation | async-start | bytes 16777216 | tf_op jit(solution)/shard_map/all_to_all | solution.py:123
  205.7 189.5 %all-to-all-start.1 = ((bf16[32,64,8,256]{3,2,1,0:T(8,128)(2,1)}), bf16[32,64,8,256]{3,2,1,0:T(8,128)(2,1)}, u32[]{:S(2)}, u32[]{:S(2)}) async-start(bf16[32,64,8,256]{3,2,1,0:T(8,128)(2,1)} %bitcast.32), calls=%async_computation.1 | async-start | bytes 16777216 | tf_op jit(solution)/shard_map/all_to_all | solution.py:123
  252.7 13.4 %copy-start.7 = (bf16[1024,2048]{0,1:T(8,128)(2,1)}, bf16[1024,2048]{0,1:T(8,128)(2,1)S(1)}, u32[]{:S(2)}) copy-start(bf16[1024,2048]{0,1:T(8,128)(2,1)S(1)} %multiply_convert_fusion) | copy-start | bytes 12582916
  266.1 4.5 copy-start.2
  395.2 190.2 %all-to-all-start.2 = ((bf16[32,64,8,256]{3,2,1,0:T(8,128)(2,1)}), bf16[32,64,8,256]{3,2,1,0:T(8,128)(2,1)}, u32[]{:S(2)}, u32[]{:S(2)}) async-start(bf16[32,64,8,256]{3,2,1,0:T(8,128)(2,1)} %bitcast.34), calls=%async_computation.2 | async-start | bytes 16777216 | tf_op jit(solution)/shard_map/all_to_all | solution.py:123
  496.5 97.3 %copy-start.4 = (s32[256]{0:T(256)S(1)}, s32[256]{0:T(256)}, u32[]{:S(2)}) copy-start(s32[256]{0:T(256)} %copy-done.3) | copy-start | bytes 3076
  496.5 97.3 %copy-start.6 = (pred[256]{0:T(512)(128)(4,1)S(1)}, pred[256]{0:T(512)(128)(4,1)}, u32[]{:S(2)}) copy-start(pred[256]{0:T(512)(128)(4,1)} %copy-done.5) | copy-start | bytes 772
  585.4 189.7 %all-to-all-start.3 = ((bf16[32,64,8,256]{3,2,1,0:T(8,128)(2,1)}), bf16[32,64,8,256]{3,2,1,0:T(8,128)(2,1)}, u32[]{:S(2)}, u32[]{:S(2)}) async-start(bf16[32,64,8,256]{3,2,1,0:T(8,128)(2,1)} %copy.10), calls=%async_computation.3 | async-start | bytes 16777216 | tf_op jit(solution)/shard_map/all_to_all | solution.py:123
  775.1 12.7 %copy-start.1 = (f32[64,256]{1,0:T(8,128)S(1)}, f32[64,256]{1,0:T(8,128)}, u32[]{:S(2)}) copy-start(f32[64,256]{1,0:T(8,128)} %param.8) | copy-start | bytes 196612
